TPU v7x, 32 devices: a whole 2x2x4 slice. The times are simulated.
32 devices in a mesh: section: 2 (over x), img: 4 (over z), ch: 4 (over y, core).
Axes of the slice: x: 2, y: 2, z: 4, core: 2. Of those that a mesh axis runs over, the one named last changes fastest.
Arguments:
- pixels: bfloat16 [8, 32, 28, 640], P('img', 'ch'), may hold values from -6 to 6
- first_gain: float32 [640], replicated, may hold values from 0.25 to 1.75
- first_shift: float32 [640], replicated, may hold values from -3 to 3
- first_kernel: bfloat16 [3, 3, 640, 640], P(None, None, 'img'), may hold values from -0.078125 to 0.078125
- projection: bfloat16 [640, 2560], P('img'), may hold values from -0.25 to 0.25
- second_gain: float32 [2560], replicated, may hold values from 0.25 to 1.75
- second_shift: float32 [2560], replicated, may hold values from -3 to 3
- second_kernel: bfloat16 [3, 3, 2560, 2560], P(None, None, ('img', 'ch')), may hold values from -0.0390625 to 0.0390625
Outputs:
- section_outputs: bfloat16 [2, 8, 16, 14, 2560], P('section', 'img', 'ch')
All inputs are finite; a program needn't handle non-finite values.
Results may differ from a plain program's by a relative error of at most 0.013.
Values may be sent and summed in bfloat16 or wider, within the bound.
No kernel may reach another device: no remote copies, remote signals or barrier semaphores. Data moves between devices by JAX's collectives and lax.ppermute only.
A program may use at most 128 MiB of HBM per device.

v0:
```python
import jax
import jax.numpy as jnp
from jax import lax
from jax.sharding import PartitionSpec as P

LAYOUT = ("NHWC", "HWIO", "NHWC")


def extended(cells, sides, width):
    for axis, dim in sides:
        count = lax.axis_size(axis)
        ends = count - 1
        head = lax.slice_in_dim(cells, 0, width, axis=dim)
        tail = lax.slice_in_dim(cells, cells.shape[dim] - width, cells.shape[dim], axis=dim)
        cells = jnp.concatenate(
            [
                lax.ppermute(tail, axis, [(i, (i + 1) % count) for i in range(ends)]),
                cells,
                lax.ppermute(head, axis, [((i + 1) % count, i) for i in range(ends)]),
            ],
            axis=dim,
        )
    return cells


def from_behind(array, axis, by):
    count = lax.axis_size(axis)
    pairs = [(i, i + by) for i in range(count) if 0 <= i + by < count]
    return lax.ppermute(array, axis, pairs)


def convolve(inputs, kernel, padding):
    return lax.conv_general_dilated(
        inputs,
        kernel,
        (1, 1),
        padding,
        dimension_numbers=LAYOUT,
        preferred_element_type=jnp.float32,
    )


def reduce_resolution(value_entries):
    count, height, breadth, depth = value_entries.shape
    blocks = value_entries.reshape(count, height // 2, 2, breadth // 2, 2, depth)
    return jnp.sum(blocks, axis=(2, 4)) * 0.25


def pick_group(value_entries, groups, shards, member):
    lead = value_entries.shape[:-1]
    per_block = value_entries.shape[-1] // (groups * shards)
    split = value_entries.reshape(lead + (groups, shards, per_block))
    chosen = lax.dynamic_slice_in_dim(split, member, 1, len(lead) + 1)
    return chosen.reshape(lead + (groups * per_block,))


def arrange_groups(value_entries, groups, shards):
    lead = value_entries.shape[:-1]
    per_block = value_entries.shape[-1] // (groups * shards)
    split = value_entries.reshape(lead + (groups, shards, per_block))
    swapped = jnp.swapaxes(split, len(lead), len(lead) + 1)
    return swapped.reshape(lead + (groups * shards * per_block,))


def body(
    pixels,
    first_gain,
    first_shift,
    first_kernel,
    projection,
    second_gain,
    second_shift,
    second_kernel,
):
    section_id = lax.axis_index("section")
    is_first = section_id == 0
    is_second = section_id == 1
    groups = lax.axis_size("img")
    shards = lax.axis_size("ch")
    member = lax.axis_index("ch")
    images, rows, columns, depth = pixels.shape
    out_rows = rows // 2
    out_cols = columns // 2
    wide = second_gain.shape[0]
    normalized_input = jax.nn.relu(pixels.astype(jnp.float32) * first_gain + first_shift).astype(
        jnp.bfloat16
    )
    padded = extended(normalized_input, (("ch", 1),), 1)
    initial_blank = jnp.zeros((images, rows, columns, depth), jnp.float32)
    piece = lax.all_gather(first_kernel, "img", axis=2, tiled=True)

    def first_compute():
        return initial_blank + convolve(padded, piece, ((0, 0), (1, 1)))

    convolved = lax.cond(is_first, first_compute, lambda: initial_blank)
    blended_result = convolved + pixels.astype(jnp.float32)
    averaged_pixels = reduce_resolution(blended_result).astype(jnp.bfloat16)
    all_rows = out_rows * shards
    flat_pooled = averaged_pixels.reshape(images * out_rows * out_cols, depth)

    def project_piece(total, piece):

        def project_compute():
            return jnp.dot(flat_pooled, piece, preferred_element_type=jnp.float32)

        return lax.cond(is_first, project_compute, lambda: total)

    proj_empty = jnp.zeros((flat_pooled.shape[0], wide), jnp.float32)
    summed_proj = project_piece(proj_empty, lax.all_gather(projection, "img", axis=0, tiled=True))
    own_rows = summed_proj.astype(jnp.bfloat16).reshape(images, out_rows, out_cols, wide)
    arrived = from_behind(own_rows, "section", 1)
    sorted_layout = arrange_groups(arrived, groups, shards)
    channel_in = lax.all_to_all(sorted_layout, "ch", split_axis=3, concat_axis=1, tiled=True)
    gain_part = pick_group(second_gain, groups, shards, member)
    shift_part = pick_group(second_shift, groups, shards, member)
    second_in = jax.nn.relu(channel_in.astype(jnp.float32) * gain_part + shift_part).astype(
        jnp.bfloat16
    )

    def second_piece(total, piece):

        def second_compute():
            return total + convolve(second_in, piece, ((1, 1), (1, 1)))

        return lax.cond(is_second, second_compute, lambda: total)

    second_empty = jnp.zeros((images, all_rows, out_cols, wide), jnp.float32)
    partial_value = second_piece(
        second_empty, lax.all_gather(second_kernel, "img", axis=2, tiled=True)
    )
    summed = lax.psum_scatter(
        partial_value.astype(jnp.bfloat16), "ch", scatter_dimension=1, tiled=True
    ).astype(jnp.float32)
    block = (summed + arrived.astype(jnp.float32)).astype(jnp.bfloat16)
    final = jnp.where(is_first, own_rows, block)
    return final[None]


def solution(mesh):
    placed = (
        P("img", "ch", None, None),
        P(),
        P(),
        P(None, None, "img", None),
        P("img", None),
        P(),
        P(),
        P(None, None, ("img", "ch"), None),
    )
    return jax.shard_map(
        body,
        mesh=mesh,
        in_specs=placed,
        out_specs=P("section", "img", "ch", None, None),
        check_vma=False,
    )
```

profile of v0, /device:TPU:0, one launch (start us, length us, event | category | flops | bytes accessed | tf_op | source)
XLA Modules:
  0.0 794.3 jit_solution(10480101129916246538)
XLA Ops:
  6.5 0.7 all-gather.4.cloned.1.call-update
  7.3 0.7 all-gather.6.cloned.1.call-update
  8.1 0.7 all-gather.8.cloned.1.call-update
  8.8 0.3 copy-done.1
  9.1 0.2 fusion.24
  9.2 0.2 fusion.30
  9.4 2.4 collective-permute-start
  11.9 1.3 collective-permute-start.1
  13.2 4.1 collective-permute-done.1
  17.2 0.7 pad_maximum_fusion
  17.9 126.7 %all-gather.4.cloned.1.call-done = bf16[3,3,640,640]{3,2,1,0:T(8,128)(2,1)} async-done(((bf16[3,3,160,640]{3,2,1,0:T(8,128)(2,1)}), bf16[3,3,640,640]{3,2,1,0:T(8,128)(2,1)}) %all-gather.4.cloned.1.call-update) | async-done | bytes 7372816 | tf_op jit(solution)/shard_map/all_gather | solution.py:90
  144.7 10.0 %conditional.3 = (f32[2,8,28,640]{3,1,2,0:T(8,128)S(1)}) conditional(s32[]{:T(128)} %convert_element_type.54, () %tuple.26, (bf16[2,10,28,640]{3,1,2,0:T(8,128)(2,1)S(1)}, bf16[3,3,640,640]{3,2,1,0:T(8,128)(2,1)}) %tuple.27), branch_computations={%region_0.1_spmd, %region_1.2_spmd} | conditional | flops 3778887680 | bytes 21739878 | solution.py:95
  144.7 0.1 copy.98
  144.8 0.2 pad
  145.0 0.2 reshape.42
  145.3 0.1 copy.75
  145.4 0.1 slice.12
  145.5 0.4 copy-done.9
  145.9 7.9 convolution_select_fusion
  153.8 0.8 copy.76
  154.7 0.1 convert_add_fusion
  154.8 0.9 copy.81
  155.7 0.6 reduce_sum.9
  156.3 0.1 multiply_convert_fusion
  156.4 53.6 %all-gather.6.cloned.1.call-done = bf16[640,2560]{1,0:T(8,128)(2,1)} async-done(((bf16[160,2560]{1,0:T(8,128)(2,1)}), bf16[640,2560]{1,0:T(8,128)(2,1)}) %all-gather.6.cloned.1.call-update) | async-done | bytes 3276816 | tf_op jit(solution)/shard_map/all_gather | solution.py:109
  210.1 3.3 conditional.4
  210.1 2.6 convolution_convert_fusion
  212.7 0.2 reshape.29
  212.9 0.4 copy.94
  213.4 1.5 collective-permute-start.2
  214.9 12.1 %collective-permute-done.2 = bf16[2,4,14,2560]{3,1,2,0:T(4,128)(2,1)S(1)} collective-permute-done((bf16[2,4,14,2560]{3,1,2,0:T(4,128)(2,1)S(1)}, bf16[2,4,14,2560]{3,1,2,0:T(4,128)(2,1)S(1)}, u32[]{:S(2)}, u32[]{:S(2)}) %collective-permute-start.2) | collective-permute-done | bytes 573472 | tf_op jit(solution)/shard_map/ppermute | solution.py:29
  227.0 1.0 reshape.36
  228.0 5.6 copy.90
  233.7 10.3 %reshape.67 = bf16[4,2,35840]{2,1,0:T(2,128)(2,1)} reshape(bf16[2560,2,4,14]{3,2,1,0:T(4,128)(2,1)} %bitcast.54) | data formatting | bytes 1146880
  244.0 3.5 all-to-all-start
  247.9 8.9 %all-to-all-done = bf16[4,2,35840]{2,1,0:T(2,128)(2,1)S(1)} async-done(((bf16[4,2,35840]{2,1,0:T(2,128)(2,1)}), bf16[4,2,35840]{2,1,0:T(2,128)(2,1)S(1)}, u32[]{:S(2)}, u32[]{:S(2)}) %all-to-all-start) | async-done | bytes 573472 | tf_op jit(solution)/shard_map/all_to_all | solution.py:113
  256.8 12.7 %reshape.68 = bf16[2560,2,4,14]{3,2,1,0:T(4,128)(2,1)} reshape(bf16[4,2,35840]{2,1,0:T(2,128)(2,1)S(1)} %all-to-all-done) | data formatting | bytes 1146880
  269.5 6.8 copy.86
  276.3 0.4 reshape.61
  276.7 0.9 copy.87
  277.6 0.8 fusion.27
  278.4 427.1 %all-gather.8.cloned.1.call-done = bf16[3,3,640,2560]{3,2,1,0:T(8,128)(2,1)} async-done(((bf16[3,3,160,2560]{3,2,1,0:T(8,128)(2,1)}), bf16[3,3,640,2560]{3,2,1,0:T(8,128)(2,1)}) %all-gather.8.cloned.1.call-update) | async-done | bytes 29491216 | tf_op jit(solution)/shard_map/all_gather | solution.py:129
  705.4 0.5 conditional.5
  705.4 0.2 broadcast_in_dim.6
  705.9 1.4 copy-done
  707.3 0.6 dynamic-slice
  708.6 76.5 %all-reduce.3.cloned.1.call-done = bf16[2,16,14,2560]{3,1,2,0:T(8,128)(2,1)} async-done(((bf16[2,16,14,2560]{3,1,2,0:T(8,128)(2,1)}), bf16[2,16,14,2560]{3,1,2,0:T(8,128)(2,1)}) %all-reduce.3.cloned.1.call-update) | async-done | bytes 2293776
  785.1 2.7 fusion.29
  (31 shorter events, 0.7 us)
Async XLA Ops:
  6.5 138.1 %all-gather.4.cloned.1.call-start = ((), (), s32[]{:S(2)}) async-start(), calls=%async_computation.1 | async-start | bytes 9216000 | tf_op jit(solution)/shard_map/all_gather | solution.py:90
  7.3 202.8 %all-gather.6.cloned.1.call-start = ((), (), s32[]{:S(2)}) async-start(), calls=%async_computation.2 | async-start | bytes 4096000 | tf_op jit(solution)/shard_map/all_gather | solution.py:109
  8.0 1.1 copy-start.1
  8.0 1.1 copy-start.6
  8.0 1.0 copy-start.7
  8.0 697.4 %all-gather.8.cloned.1.call-start = ((), (), s32[]{:S(2)}) async-start(), calls=%async_computation.3 | async-start | bytes 36864000 | tf_op jit(solution)/shard_map/all_gather | solution.py:129
  9.4 3.7 collective-permute-start
  11.9 5.4 collective-permute-start.1
  145.2 0.7 copy-start.9
  213.4 20.3 %copy-start.2 = (bf16[2,4,14,2560]{3,1,2,0:T(4,128)(2,1)}, bf16[2,4,14,2560]{3,1,2,0:T(4,128)(2,1)S(1)}, u32[]{:S(2)}) copy-start(bf16[2,4,14,2560]{3,1,2,0:T(4,128)(2,1)S(1)} %get-tuple-element.60) | copy-start | bytes 1720324
  213.4 13.6 %collective-permute-start.2 = (bf16[2,4,14,2560]{3,1,2,0:T(4,128)(2,1)S(1)}, bf16[2,4,14,2560]{3,1,2,0:T(4,128)(2,1)S(1)}, u32[]{:S(2)}, u32[]{:S(2)}) collective-permute-start(bf16[2,4,14,2560]{3,1,2,0:T(4,128)(2,1)S(1)} %get-tuple-element.60), channel_id=1, source_target_pairs={{0,16},{1,17},{2,18},{3,19},{4,20},{5,21},{6,22},{7,23},{8,24},{9,... | collective-permute-start | bytes 1720328 | tf_op jit(solution)/shard_map/ppermute | solution.py:29
  233.7 13.8 %copy-start.4 = (f32[2560]{0:T(1024)S(1)}, f32[2560]{0:T(1024)}, u32[]{:S(2)}) copy-start(f32[2560]{0:T(1024)} %param.19) | copy-start | bytes 30724
  233.7 13.9 %copy-start.5 = (f32[2560]{0:T(1024)S(1)}, f32[2560]{0:T(1024)}, u32[]{:S(2)}) copy-start(f32[2560]{0:T(1024)} %param.20) | copy-start | bytes 30724
  244.0 12.8 %all-to-all-start = ((bf16[4,2,35840]{2,1,0:T(2,128)(2,1)}), bf16[4,2,35840]{2,1,0:T(2,128)(2,1)S(1)}, u32[]{:S(2)}, u32[]{:S(2)}) async-start(bf16[4,2,35840]{2,1,0:T(2,128)(2,1)} %reshape.67), calls=%async_computation | async-start | bytes 1146880 | tf_op jit(solution)/shard_map/all_to_all | solution.py:113
  247.4 537.6 %all-reduce.3.cloned.1.call-start = ((), (), s32[]{:S(2)}) async-start(), calls=%async_computation.4 | async-start | bytes 4587520
  705.9 1.4 copy-start
  705.9 1.4 copy-start.8
  705.9 79.2 %copy-start.3 = (bf16[2,4,14,2560]{3,1,2,0:T(4,128)(2,1)S(1)}, bf16[2,4,14,2560]{3,1,2,0:T(4,128)(2,1)}, u32[]{:S(2)}) copy-start(bf16[2,4,14,2560]{3,1,2,0:T(4,128)(2,1)} %copy-done.2) | copy-start | bytes 1720324
Sparse Core Ops, SparseCore 0:
  8.9 135.7 all-gather.3
  146.2 63.7 all-gather.5
  211.6 493.7 all-gather.7
  707.7 77.3 all-reduce.2
where the time goes:
time: 795 us; the launch traced here: 794 us
  waiting for transfers between devices  711 us (89%)
  local copies, waits for them, and re-layouts  44.5 us (6%)
  between operations  14 us (2%)
  matrix products  10.5 us (1%)
  starting transfers between devices  8.8 us (1%)
    all_gather x1, waiting for transfers between devices, body(): lax.all_gather(second_kernel, 'img', axis=2, tiled=True)  427 us
    all_gather x1, waiting for transfers between devices, body(): piece = lax.all_gather(first_kernel, 'img', axis=2, tiled=True)  127 us
    unnamed x5, waiting for transfers between devices  78.6 us
    all_gather x1, waiting for transfers between devices, body(): lax.all_gather(projection, 'img', axis=0, tiled=True)  53.6 us
    unnamed x21, local copies, waits for them, and re-layouts  25.4 us
  transfers between devices with their start and end apart: 8, of which 7 were waited for; matrix products, arithmetic and copies ran while one was open for 7% of the time, Pallas kernels for 0%

commit v1 on v0

--- a/solution.py
+++ b/solution.py
@@ -4,6 +4,19 @@
 from jax.sharding import PartitionSpec as P
 
 LAYOUT = ("NHWC", "HWIO", "NHWC")
+
+
+def collect(x, axis, dim):
+    ways = lax.axis_size(axis)
+    up = [(d, (d + 1) % ways) for d in range(ways)]
+    down = [(d, (d - 1) % ways) for d in range(ways)]
+    earlier, later = ([x], [x])
+    for _ in range(ways // 2):
+        earlier.append(lax.ppermute(earlier[-1], axis, up))
+    for _ in range((ways - 1) // 2):
+        later.append(lax.ppermute(later[-1], axis, down))
+    line = jnp.concatenate([*earlier[::-1], *later[1:]], axis=dim)
+    return jnp.roll(line, (lax.axis_index(axis) - ways // 2) * x.shape[dim], axis=dim)
 
 
 def extended(cells, sides, width):
@@ -106,7 +119,7 @@
         return lax.cond(is_first, project_compute, lambda: total)
 
     proj_empty = jnp.zeros((flat_pooled.shape[0], wide), jnp.float32)
-    summed_proj = project_piece(proj_empty, lax.all_gather(projection, "img", axis=0, tiled=True))
+    summed_proj = project_piece(proj_empty, collect(projection, "img", 0))
     own_rows = summed_proj.astype(jnp.bfloat16).reshape(images, out_rows, out_cols, wide)
     arrived = from_behind(own_rows, "section", 1)
     sorted_layout = arrange_groups(arrived, groups, shards)

time: 795 us -> 771 us (0.970)
  waiting for transfers between devices: 711 us -> 659 us
  local copies, waits for them, and re-layouts: 44.5 us -> 58.8 us
  starting transfers between devices: 8.8 us -> 21.2 us
    ppermute x0 -> x3, waiting for transfers between devices: none -> 86.7 us  [the longest x2 57 us: collect(): earlier.append(lax.ppermute(earlier[-1], axis, up))]
    all_gather x1, waiting for transfers between devices: 127 us -> 55.4 us  [body(): piece = lax.all_gather(first_kernel, 'img', axis=2, tiled=True)]
    all_gather x1 -> x0, waiting for transfers between devices: 53.6 us -> none  [body(): lax.all_gather(projection, 'img', axis=0, tiled=True)]
    ppermute x0 -> x3, starting transfers between devices: none -> 13.6 us  [the longest x2 13.5 us: collect(): earlier.append(lax.ppermute(earlier[-1], axis, up))]
    all_gather x1, waiting for transfers between devices: 427 us -> 414 us  [body(): lax.all_gather(second_kernel, 'img', axis=2, tiled=True)]
    unnamed x21 -> x32, local copies, waits for them, and re-layouts: 25.4 us -> 37.7 us
    unnamed x5 -> x4, waiting for transfers between devices: 78.6 us -> 77.8 us
  transfers between devices with their start and end apart: 8 -> 10, of which waited for: 7 -> 9; matrix products, arithmetic and copies ran while one was open for 7% -> 9% of each run, Pallas kernels for 0% -> 0%
where the time goes in v1:
time: 771 us; the launch traced here: 770 us
  waiting for transfers between devices  659 us (85%)
  local copies, waits for them, and re-layouts  58.8 us (8%)
  starting transfers between devices  21.2 us (3%)
  between operations  13.9 us (2%)
  matrix products  11.8 us (2%)
    all_gather x1, waiting for transfers between devices, body(): lax.all_gather(second_kernel, 'img', axis=2, tiled=True)  414 us
    unnamed x4, waiting for transfers between devices  77.8 us
    ppermute x2, waiting for transfers between devices, collect(): earlier.append(lax.ppermute(earlier[-1], axis, up))  57 us
    all_gather x1, waiting for transfers between devices, body(): piece = lax.all_gather(first_kernel, 'img', axis=2, tiled=True)  55.4 us
    unnamed x32, local copies, waits for them, and re-layouts  37.7 us
    ppermute x1, waiting for transfers between devices, collect(): later.append(lax.ppermute(later[-1], axis, down))  29.7 us
  transfers between devices with their start and end apart: 10, of which 9 were waited for; matrix products, arithmetic and copies ran while one was open for 9% of the time, Pallas kernels for 0%

profile of v1, /device:TPU:0, one launch (start us, length us, event | category | flops | bytes accessed | tf_op | source)
XLA Modules:
  0.0 770.5 jit_solution(857650705995649198)
XLA Ops:
  6.5 0.7 all-gather.3.cloned.1.call-update
  7.3 0.7 all-gather.5.cloned.1.call-update
  8.0 0.4 copy-done.1
  8.4 3.1 collective-permute-start
  11.5 27.6 %collective-permute-done = bf16[160,2560]{1,0:T(8,128)(2,1)} collective-permute-done((bf16[160,2560]{1,0:T(8,128)(2,1)S(1)}, bf16[160,2560]{1,0:T(8,128)(2,1)}, u32[]{:S(2)}, u32[]{:S(2)}) %collective-permute-start) | collective-permute-done | bytes 819232 | tf_op jit(solution)/shard_map/ppermute | solution.py:15
  39.1 10.4 %collective-permute-start.1 = (bf16[160,2560]{1,0:T(8,128)(2,1)}, bf16[160,2560]{1,0:T(8,128)(2,1)}, u32[]{:S(2)}, u32[]{:S(2)}) collective-permute-start(bf16[160,2560]{1,0:T(8,128)(2,1)} %collective-permute-done), channel_id=1, source_target_pairs={{0,4},{4,8},{8,12},{12,0},{1,5},{5,9},{9,13},{13,1},{2,6},{6,10},{... | collective-permute-start | bytes 2457608 | tf_op jit(solution)/shard_map/ppermute | solution.py:15
  49.9 1.3 collective-permute-start.3
  51.2 1.3 collective-permute-start.4
  52.6 3.5 collective-permute-done.4
  56.1 0.7 pad_maximum_fusion
  56.8 29.4 %collective-permute-done.1 = bf16[160,2560]{1,0:T(8,128)(2,1)} collective-permute-done((bf16[160,2560]{1,0:T(8,128)(2,1)}, bf16[160,2560]{1,0:T(8,128)(2,1)}, u32[]{:S(2)}, u32[]{:S(2)}) %collective-permute-start.1) | collective-permute-done | bytes 819232 | tf_op jit(solution)/shard_map/ppermute | solution.py:15
  86.2 2.1 constant_dynamic-update-slice_fusion.7
  88.4 2.1 constant_dynamic-update-slice_fusion.6
  90.5 0.9 constant_dynamic-update-slice_fusion.5
  91.4 29.7 %collective-permute-done.2 = bf16[160,2560]{1,0:T(8,128)(2,1)} collective-permute-done((bf16[160,2560]{1,0:T(8,128)(2,1)S(1)}, bf16[160,2560]{1,0:T(8,128)(2,1)}, u32[]{:S(2)}, u32[]{:S(2)}) %collective-permute-start.2) | collective-permute-done | bytes 819232 | tf_op jit(solution)/shard_map/ppermute | solution.py:17
  121.1 2.1 constant_dynamic-update-slice_fusion.4
  123.2 2.1 constant_dynamic-update-slice_fusion.3
  125.3 2.2 constant_dynamic-update-slice_fusion.2
  127.5 0.9 constant_dynamic-update-slice_fusion.1
  128.4 2.1 constant_dynamic-update-slice_fusion
  130.5 55.4 %all-gather.3.cloned.1.call-done = bf16[3,3,640,640]{3,2,1,0:T(8,128)(2,1)} async-done(((bf16[3,3,160,640]{3,2,1,0:T(8,128)(2,1)}), bf16[3,3,640,640]{3,2,1,0:T(8,128)(2,1)}) %all-gather.3.cloned.1.call-update) | async-done | bytes 7372816 | tf_op jit(solution)/shard_map/all_gather | solution.py:103
  186.0 9.8 %conditional.3 = (f32[2,8,28,640]{3,1,2,0:T(8,128)S(1)}) conditional(s32[]{:T(128)} %convert_element_type.60, () %tuple.38, (bf16[2,10,28,640]{3,1,2,0:T(8,128)(2,1)S(1)}, bf16[3,3,640,640]{3,2,1,0:T(8,128)(2,1)}) %tuple.39), branch_computations={%region_0.1_spmd, %region_1.2_spmd} | conditional | flops 3778887680 | bytes 21739878 | solution.py:108
  187.0 7.9 %convolution_select_fusion = f32[8,16,4,640]{3,1,2,0:T(8,128)S(1)} fusion(bf16[3,3,640,640]{3,2,1,0:T(8,128)(2,1)} %get-tuple-element.102, bf16[10,2,7,2,640]{4,2,1,3,0:T(8,128)(2,1)S(1)} %slice.12, bf16[10,2,8,4,640]{4,2,1,3,0:T(8,128)(2,1)S(1)} %copy.75, pred[16,4]{0,1:T(4,128)(4,1)S(1)} %copy-done.11), kind=kOutput, calls=%fused_computation.2 | convolution fusion | flops 3778887680 | bytes 9861184 | tf_op jit(solution)/shard_map/cond/branch_1_fun/conv_general_dilated | solution.py:46
  194.9 0.8 copy.76
  195.9 0.9 copy.81
  196.8 0.6 reduce_sum.9
  197.6 4.7 conditional.4
  197.7 3.9 fusion.11
  201.8 0.4 copy.94
  202.3 1.5 collective-permute-start.5
  203.8 12.5 %collective-permute-done.5 = bf16[2,4,14,2560]{3,1,2,0:T(4,128)(2,1)S(1)} collective-permute-done((bf16[2,4,14,2560]{3,1,2,0:T(4,128)(2,1)S(1)}, bf16[2,4,14,2560]{3,1,2,0:T(4,128)(2,1)S(1)}, u32[]{:S(2)}, u32[]{:S(2)}) %collective-permute-start.5) | collective-permute-done | bytes 573472 | tf_op jit(solution)/shard_map/ppermute | solution.py:42
  216.3 1.0 reshape.39
  217.3 5.7 copy.90
  223.0 10.2 %reshape.70 = bf16[4,2,35840]{2,1,0:T(2,128)(2,1)} reshape(bf16[2560,2,4,14]{3,2,1,0:T(4,128)(2,1)} %bitcast.55) | data formatting | bytes 1146880
  233.1 3.5 all-to-all-start
  237.0 8.9 %all-to-all-done = bf16[4,2,35840]{2,1,0:T(2,128)(2,1)S(1)} async-done(((bf16[4,2,35840]{2,1,0:T(2,128)(2,1)}), bf16[4,2,35840]{2,1,0:T(2,128)(2,1)S(1)}, u32[]{:S(2)}, u32[]{:S(2)}) %all-to-all-start) | async-done | bytes 573472 | tf_op jit(solution)/shard_map/all_to_all | solution.py:126
  245.9 12.7 %reshape.71 = bf16[2560,2,4,14]{3,2,1,0:T(4,128)(2,1)} reshape(bf16[4,2,35840]{2,1,0:T(2,128)(2,1)S(1)} %all-to-all-done) | data formatting | bytes 1146880
  258.7 6.8 copy.86
  265.5 0.4 reshape.64
  265.9 0.9 copy.87
  266.7 0.8 fusion.30
  267.5 414.4 %all-gather.5.cloned.1.call-done = bf16[3,3,640,2560]{3,2,1,0:T(8,128)(2,1)} async-done(((bf16[3,3,160,2560]{3,2,1,0:T(8,128)(2,1)}), bf16[3,3,640,2560]{3,2,1,0:T(8,128)(2,1)}) %all-gather.5.cloned.1.call-update) | async-done | bytes 29491216 | tf_op jit(solution)/shard_map/all_gather | solution.py:142
  681.9 0.5 conditional.5
  681.9 0.2 broadcast_in_dim.6
  682.4 1.4 copy-done
  683.8 0.6 dynamic-slice
  684.9 76.4 %all-reduce.3.cloned.1.call-done = bf16[2,16,14,2560]{3,1,2,0:T(8,128)(2,1)} async-done(((bf16[2,16,14,2560]{3,1,2,0:T(8,128)(2,1)}), bf16[2,16,14,2560]{3,1,2,0:T(8,128)(2,1)}) %all-reduce.3.cloned.1.call-update) | async-done | bytes 2293776
  761.3 2.7 fusion.32
  (46 shorter events, 2.5 us)
Async XLA Ops:
  6.5 179.4 %all-gather.3.cloned.1.call-start = ((), (), s32[]{:S(2)}) async-start(), calls=%async_computation.1 | async-start | bytes 9216000 | tf_op jit(solution)/shard_map/all_gather | solution.py:103
  7.3 1.1 copy-start.1
  7.3 42.3 %copy-start.2 = (bf16[2,8,28,640]{3,1,2,0:T(8,128)(2,1)S(1)}, bf16[2,8,28,640]{3,1,2,0:T(8,128)(2,1)}, u32[]{:S(2)}) copy-start(bf16[2,8,28,640]{3,1,2,0:T(8,128)(2,1)} %param.14) | copy-start | bytes 1720324
  7.3 42.3 %copy-start.8 = (f32[640]{0:T(1024)S(1)}, f32[640]{0:T(1024)}, u32[]{:S(2)}) copy-start(f32[640]{0:T(1024)} %param.16) | copy-start | bytes 7684
  7.3 42.3 %copy-start.9 = (f32[640]{0:T(1024)S(1)}, f32[640]{0:T(1024)}, u32[]{:S(2)}) copy-start(f32[640]{0:T(1024)} %param.15) | copy-start | bytes 7684
  7.3 674.6 %all-gather.5.cloned.1.call-start = ((), (), s32[]{:S(2)}) async-start(), calls=%async_computation.2 | async-start | bytes 36864000 | tf_op jit(solution)/shard_map/all_gather | solution.py:142
  8.4 30.7 %collective-permute-start = (bf16[160,2560]{1,0:T(8,128)(2,1)S(1)}, bf16[160,2560]{1,0:T(8,128)(2,1)}, u32[]{:S(2)}, u32[]{:S(2)}) collective-permute-start(bf16[160,2560]{1,0:T(8,128)(2,1)S(1)} %copy-done.1), channel_id=1, source_target_pairs={{0,4},{4,8},{8,12},{12,0},{1,5},{5,9},{9,13},{13,1},{2,6},{6,10},{... | collective-permute-start | bytes 2457608 | tf_op jit(solution)/shard_map/ppermute | solution.py:15
  39.1 47.1 %collective-permute-start.1 = (bf16[160,2560]{1,0:T(8,128)(2,1)}, bf16[160,2560]{1,0:T(8,128)(2,1)}, u32[]{:S(2)}, u32[]{:S(2)}) collective-permute-start(bf16[160,2560]{1,0:T(8,128)(2,1)} %collective-permute-done), channel_id=1, source_target_pairs={{0,4},{4,8},{8,12},{12,0},{1,5},{5,9},{9,13},{13,1},{2,6},{6,10},{... | collective-permute-start | bytes 2457608 | tf_op jit(solution)/shard_map/ppermute | solution.py:15
  49.9 2.7 collective-permute-start.3
  51.2 4.9 collective-permute-start.4
  52.5 68.6 %collective-permute-start.2 = (bf16[160,2560]{1,0:T(8,128)(2,1)S(1)}, bf16[160,2560]{1,0:T(8,128)(2,1)}, u32[]{:S(2)}, u32[]{:S(2)}) collective-permute-start(bf16[160,2560]{1,0:T(8,128)(2,1)S(1)} %copy-done.1), channel_id=1, source_target_pairs={{0,12},{4,0},{8,4},{12,8},{1,13},{5,1},{9,5},{13,9},{2,14},{6,2},{... | collective-permute-start | bytes 2457608 | tf_op jit(solution)/shard_map/ppermute | solution.py:17
  186.0 9.8 %copy-start.3 = (bf16[2,8,28,640]{3,1,2,0:T(8,128)(2,1)S(1)}, bf16[2,8,28,640]{3,1,2,0:T(8,128)(2,1)}, u32[]{:S(2)}) copy-start(bf16[2,8,28,640]{3,1,2,0:T(8,128)(2,1)} %param.14) | copy-start | bytes 1720324
  186.4 0.7 copy-start.11
  202.2 20.7 %copy-start.4 = (bf16[2,4,14,2560]{3,1,2,0:T(4,128)(2,1)}, bf16[2,4,14,2560]{3,1,2,0:T(4,128)(2,1)S(1)}, u32[]{:S(2)}) copy-start(bf16[2,4,14,2560]{3,1,2,0:T(4,128)(2,1)S(1)} %get-tuple-element.138) | copy-start | bytes 1720324
  202.3 14.0 %collective-permute-start.5 = (bf16[2,4,14,2560]{3,1,2,0:T(4,128)(2,1)S(1)}, bf16[2,4,14,2560]{3,1,2,0:T(4,128)(2,1)S(1)}, u32[]{:S(2)}, u32[]{:S(2)}) collective-permute-start(bf16[2,4,14,2560]{3,1,2,0:T(4,128)(2,1)S(1)} %get-tuple-element.138), channel_id=1, source_target_pairs={{0,16},{1,17},{2,18},{3,19},{4,20},{5,21},{6,22},{7,23},{8,24},{9,... | collective-permute-start | bytes 1720328 | tf_op jit(solution)/shard_map/ppermute | solution.py:42
  223.0 13.7 %copy-start.6 = (f32[2560]{0:T(1024)S(1)}, f32[2560]{0:T(1024)}, u32[]{:S(2)}) copy-start(f32[2560]{0:T(1024)} %param.19) | copy-start | bytes 30724
  223.0 13.8 %copy-start.7 = (f32[2560]{0:T(1024)S(1)}, f32[2560]{0:T(1024)}, u32[]{:S(2)}) copy-start(f32[2560]{0:T(1024)} %param.20) | copy-start | bytes 30724
  233.1 12.8 %all-to-all-start = ((bf16[4,2,35840]{2,1,0:T(2,128)(2,1)}), bf16[4,2,35840]{2,1,0:T(2,128)(2,1)S(1)}, u32[]{:S(2)}, u32[]{:S(2)}) async-start(bf16[4,2,35840]{2,1,0:T(2,128)(2,1)} %reshape.70), calls=%async_computation | async-start | bytes 1146880 | tf_op jit(solution)/shard_map/all_to_all | solution.py:126
  236.6 524.7 %all-reduce.3.cloned.1.call-start = ((), (), s32[]{:S(2)}) async-start(), calls=%async_computation.3 | async-start | bytes 4587520
  682.4 1.4 copy-start
  682.4 1.4 copy-start.10
  682.4 78.9 %copy-start.5 = (bf16[2,4,14,2560]{3,1,2,0:T(4,128)(2,1)S(1)}, bf16[2,4,14,2560]{3,1,2,0:T(4,128)(2,1)}, u32[]{:S(2)}) copy-start(bf16[2,4,14,2560]{3,1,2,0:T(4,128)(2,1)} %copy-done.4) | copy-start | bytes 1720324
Sparse Core Ops, SparseCore 0:
  8.9 177.0 all-gather.2
  187.6 494.2 all-gather.4
  684.3 76.9 all-reduce.2
